TPU v7x, 128 devices: a whole 4x4x4 slice. The times are simulated.
128 devices in a mesh: rep: 32 (over x, y, core), grp: 4 (over z).
Axes of the slice: x: 4, y: 4, z: 4, core: 2. Of those that a mesh axis runs over, the one named last changes fastest.
Arguments:
- grads: bfloat16 [128, 2, 320, 2048], P(('rep', 'grp')), may hold values from -6 to 6
- errors: float32 [128, 2, 320, 2048], P(('rep', 'grp')), may hold values from -4 to 4
- warm_start: float32 [2, 32, 2048], replicated, may hold values from -0.125 to 0.125
- vec_grads: float32 [128, 2, 2048], P(('rep', 'grp')), may hold values from -6 to 6
- owners: int32 [12], replicated, may hold values from 0 to 127, as said below
- mat_momentum: float32 [256, 64, 2048], P(('rep', 'grp')), may hold values from -0.3 to 0.3
- mat_weights: float32 [256, 64, 2048], P(('rep', 'grp')), may hold values from -0.3 to 0.3
- vec_momentum: float32 [256, 2048], P(('rep', 'grp')), may hold values from -0.3 to 0.3
- vec_weights: float32 [256, 2048], P(('rep', 'grp')), may hold values from 0.5 to 1.5
Outputs:
- new_errors: float32 [128, 2, 320, 2048], P(('rep', 'grp'))
- mat_momentum_out: float32 [256, 64, 2048], P(('rep', 'grp'))
- mat_weights_out: float32 [256, 64, 2048], P(('rep', 'grp'))
- vec_momentum_out: float32 [256, 2048], P(('rep', 'grp'))
- vec_weights_out: float32 [256, 2048], P(('rep', 'grp'))
Inputs may be any that keep to these rules, and one draw needn't show every extreme that they name: `owners`: no replica owns more than 2 items, and some replica owns exactly 2. Replicas 0 and 127 each own at least one item.
All inputs are finite; a program needn't handle non-finite values.
Results may differ from a plain program's by a relative error of at most 0.0003.
Values sent between devices are 32-bit elements; how exact they have to be, the bound alone decides.
A program may use at most 64 MiB of HBM per device.

v0:
```python
import jax
import jax.numpy as jnp
from jax import lax
from jax.sharding import PartitionSpec as P

ROOT_ITERS = 12


high = lax.Precision.HIGHEST


def orthonormal(factor):
    gram_matrix = jnp.einsum("mkr,mks->mrs", factor, factor, precision=high)
    spread = jnp.sqrt(jnp.sum(gram_matrix * gram_matrix, axis=(1, 2)))[:, None, None]
    identity_mat = jnp.broadcast_to(
        jnp.eye(gram_matrix.shape[1], dtype=jnp.float32), gram_matrix.shape
    )
    root_left = gram_matrix / spread
    root_right = identity_mat
    for sweep in range(ROOT_ITERS):
        middle = 1.5 * identity_mat - 0.5 * jnp.einsum(
            "mrs,mst->mrt", root_right, root_left, precision=high
        )
        root_left = jnp.einsum("mrs,mst->mrt", root_left, middle, precision=high)
        root_right = jnp.einsum("mrs,mst->mrt", middle, root_right, precision=high)
    return jnp.einsum("mkr,mrs->mks", factor, root_right, precision=high) / jnp.sqrt(spread)


def replicas_total(partial_term):
    return lax.psum(partial_term, ("rep", "grp"))


def local(
    grads,
    errors,
    warm_start,
    vec_grads,
    owners,
    mat_momentum,
    mat_weights,
    vec_momentum,
    vec_weights,
):
    count = lax.axis_size("rep") * lax.axis_size("grp")
    combined = grads[0].astype(jnp.float32) + errors[0]
    first_term = jnp.einsum("mkd,mrd->mkr", combined, warm_start, precision=high)
    p_sum = lax.psum(first_term, ("rep", "grp"))
    p_hat = orthonormal(p_sum / count)
    q_factor = replicas_total(jnp.einsum("mks,mkd->msd", p_hat, combined, precision=high)) / count
    p_sum = replicas_total(jnp.einsum("mkd,mrd->mkr", combined, q_factor, precision=high))
    p_hat = orthonormal(p_sum / count)
    q_factor = replicas_total(jnp.einsum("mks,mkd->msd", p_hat, combined, precision=high)) / count
    approx = jnp.einsum("mks,msd->mkd", p_hat, q_factor, precision=high)
    new_errors = (combined - approx)[None]
    vec_sum = lax.psum(vec_grads[0], ("rep", "grp"))
    vec_avg = vec_sum / count
    device = lax.axis_index("rep") * lax.axis_size("grp") + lax.axis_index("grp")
    items = owners.shape[0]
    earlier = jnp.arange(items)[None, :] < jnp.arange(items)[:, None]
    same = owners[None, :] == owners[:, None]
    slot = jnp.sum((earlier & same).astype(jnp.int32), axis=1)
    slot_count = mat_momentum.shape[0]
    match = (owners[None, :] == device) & (slot[None, :] == jnp.arange(slot_count)[:, None])
    match = match.astype(jnp.float32)
    head_items = approx.shape[0] * (approx.shape[1] // mat_momentum.shape[1])
    mat_match = match[:, :head_items]
    vec_match = match[:, head_items:]
    blocks = approx.reshape(head_items, mat_momentum.shape[1], approx.shape[2])
    picked = jnp.einsum("si,ihd->shd", mat_match, blocks, precision=high)
    has_block = jnp.sum(mat_match, axis=1) > 0.5
    moment = 0.9 * mat_momentum + picked
    mat_momentum_out = jnp.where(has_block[:, None, None], moment, mat_momentum)
    mat_weights_out = jnp.where(has_block[:, None, None], mat_weights - 0.5 * moment, mat_weights)
    picked_vec = jnp.dot(vec_match, vec_avg, precision=high)
    has_vec = jnp.sum(vec_match, axis=1) > 0.5
    vec_moment = 0.9 * vec_momentum + picked_vec
    vec_momentum_out = jnp.where(has_vec[:, None], vec_moment, vec_momentum)
    vec_weights_out = jnp.where(has_vec[:, None], vec_weights - 0.5 * vec_moment, vec_weights)
    return (new_errors, mat_momentum_out, mat_weights_out, vec_momentum_out, vec_weights_out)


def solution(mesh):
    placed = (
        P(("rep", "grp"), None, None, None),
        P(("rep", "grp"), None, None, None),
        P(),
        P(("rep", "grp"), None, None),
        P(),
        P(("rep", "grp"), None, None),
        P(("rep", "grp"), None, None),
        P(("rep", "grp"), None),
        P(("rep", "grp"), None),
    )
    return jax.shard_map(
        local,
        mesh=mesh,
        in_specs=placed,
        out_specs=(
            P(("rep", "grp"), None, None, None),
            P(("rep", "grp"), None, None),
            P(("rep", "grp"), None, None),
            P(("rep", "grp"), None),
            P(("rep", "grp"), None),
        ),
        check_vma=False,
    )
```

profile of v0, /device:TPU:1, one launch (start us, length us, event | category | flops | bytes accessed | tf_op | source)
XLA Modules:
  0.0 650.4 jit_solution(16320560180728181327)
XLA Ops:
  7.2 1.0 copy-done
  8.2 7.8 %fusion.8 = f32[2,320,32]{1,2,0:T(8,128)} fusion(f32[2,32,2048]{2,1,0:T(8,128)S(1)} %copy-done, f32[1,2,320,2048]{3,2,1,0:T(8,128)} %param.10, bf16[1,2,320,2048]{3,2,1,0:T(8,128)(2,1)} %param.9), kind=kOutput, calls=%fused_computation.9 | convolution fusion | flops 505937920 | bytes 8470528 | tf_op jit(solution)/shard_map/mkd,mrd->mkr/dot_general | solution.py:46
  16.2 0.2 convert_reduce_fusion
  16.4 141.4 %all-reduce.5.cloned.1.call-done = f32[2,320,32]{1,2,0:T(8,128)} async-done(((f32[2,320,32]{1,2,0:T(8,128)}), f32[2,320,32]{1,2,0:T(8,128)}) %all-reduce.5.cloned.1.call-update) | async-done | bytes 81936 | tf_op jit(solution)/shard_map/psum | solution.py:47
  157.8 1.3 multiply_reduce_fusion.1
  159.1 0.2 fusion.37
  159.4 0.2 fusion.64
  159.8 0.2 fusion.36
  161.8 0.2 fusion.32
  162.8 0.2 fusion.30
  165.2 1.6 convolution_divide_fusion
  166.8 6.8 %fusion.6 = f32[2,32,2048]{2,1,0:T(8,128)} fusion(f32[2,320,32]{2,1,0:T(8,128)S(1)} %convolution_divide_fusion, f32[1,2,320,2048]{3,2,1,0:T(8,128)} %param.10, bf16[1,2,320,2048]{3,2,1,0:T(8,128)(2,1)S(1)} %copy-done.1), kind=kOutput, calls=%fused_computation.7 | convolution fusion | flops 505937920 | bytes 8470528 | tf_op jit(solution)/shard_map/mks,mkd->msd/dot_general | solution.py:49
  173.6 0.2 all-reduce.9.cloned.1.call-start
  173.9 142.2 %all-reduce.7.cloned.1.call-done = f32[2,32,2048]{2,1,0:T(8,128)} async-done(((f32[2,32,2048]{2,1,0:T(8,128)}), f32[2,32,2048]{2,1,0:T(8,128)}) %all-reduce.7.cloned.1.call-update) | async-done | bytes 524304 | tf_op jit(solution)/shard_map/psum | solution.py:30
  316.2 8.3 %fusion.4 = f32[2,320,32]{1,2,0:T(8,128)} fusion(f32[2,32,2048]{2,1,0:T(8,128)} %all-reduce.7.cloned.1.call-done, f32[1,2,320,2048]{3,2,1,0:T(8,128)} %param.10, bf16[1,2,320,2048]{3,2,1,0:T(8,128)(2,1)S(1)} %copy-done.1), kind=kOutput, calls=%fused_computation.5 | convolution fusion | flops 506068992 | bytes 8470528 | tf_op jit(solution)/shard_map/mkd,mrd->mkr/dot_general | solution.py:50
  324.5 0.2 slice_reduce_fusion
  324.7 136.8 %all-reduce.9.cloned.1.call-done = f32[2,320,32]{1,2,0:T(8,128)} async-done(((f32[2,320,32]{1,2,0:T(8,128)}), f32[2,320,32]{1,2,0:T(8,128)}) %all-reduce.9.cloned.1.call-update) | async-done | bytes 81936 | tf_op jit(solution)/shard_map/psum | solution.py:30
  461.5 1.3 multiply_reduce_fusion
  462.8 0.2 fusion.25
  463.1 0.2 fusion.65
  463.5 0.2 fusion.24
  468.8 0.2 fusion.118
  469.0 1.1 convolution_divide_fusion.1
  470.1 6.7 %fusion.2 = f32[2,32,2048]{2,1,0:T(8,128)} fusion(f32[2,320,32]{1,2,0:T(8,128)S(1)} %convolution_divide_fusion.1, f32[1,2,320,2048]{3,2,1,0:T(8,128)} %param.10, bf16[1,2,320,2048]{3,2,1,0:T(8,128)(2,1)S(1)} %copy-done.1), kind=kOutput, calls=%fused_computation.3 | convolution fusion | flops 505937920 | bytes 8470528 | tf_op jit(solution)/shard_map/mks,mkd->msd/dot_general | solution.py:52
  476.8 63.6 %psum.39 = f32[2,2048]{1,0:T(2,128)S(1)} all-reduce(f32[2,2048]{1,0:T(2,128)S(1)} %bitcast.160), channel_id=1, replica_groups=mesh['rep'=32,'grp'=4] {'rep','grp'}, use_global_device_ids=true, to_apply=%region_9.10 | all-reduce | flops 4096 | bytes 32768 | tf_op jit(solution)/shard_map/psum | solution.py:55
  540.4 0.8 subtract_select_fusion.1
  541.2 78.4 %all-reduce.11.cloned.1.call-done = f32[2,32,2048]{2,1,0:T(8,128)} async-done(((f32[2,32,2048]{2,1,0:T(8,128)}), f32[2,32,2048]{2,1,0:T(8,128)}) %all-reduce.11.cloned.1.call-update) | async-done | bytes 524304 | tf_op jit(solution)/shard_map/psum | solution.py:30
  619.6 5.4 fusion.38
  625.0 6.5 fusion.10
  631.5 9.2 %subtract_select_fusion = (f32[2,64,2048]{2,0,1:T(2,128)S(1)}, f32[2,64,2048]{2,0,1:T(2,128)S(1)}) fusion(f32[2,64,2048]{2,1,0:T(8,128)S(1)} %copy-done.2, pred[2]{0:T(512)(128)(4,1)S(1)} %broadcast_compare_fusion.1, f32[2,64,2048]{2,1,0:T(8,128)S(1)} %copy-done.3, f32[10,64,2048]{2,1,0:T(8,128)S(1)} %bitcast.159, pred[2,12]{1,0:T(4,128)(4,1)S(1)} %get-tuple-element.16), kind=kOutput, calls=%fused_computation.15 | convolution fusion | flops 33030144 | bytes 9437210 | tf_op jit(solution)/shard_map/si,ihd->shd/dot_general | solution.py:69
  640.7 1.6 copy.27
  642.3 1.6 copy.26
  (92 shorter events, 10.2 us)
Async XLA Ops:
  7.2 1.0 copy-start
  7.2 159.6 %copy-start.1 = (bf16[1,2,320,2048]{3,2,1,0:T(8,128)(2,1)S(1)}, bf16[1,2,320,2048]{3,2,1,0:T(8,128)(2,1)}, u32[]{:S(2)}) copy-start(bf16[1,2,320,2048]{3,2,1,0:T(8,128)(2,1)} %param.9) | copy-start | bytes 7864324
  7.2 9.0 %copy-start.7 = (s32[12]{0:T(128)S(1)}, s32[12]{0:T(128)}, u32[]{:S(2)}) copy-start(s32[12]{0:T(128)} %param.13) | copy-start | bytes 148
  7.2 150.6 %all-reduce.5.cloned.1.call-start = ((), (), s32[]{:S(2)}) async-start(), calls=%async_computation | async-start | bytes 196608 | tf_op jit(solution)/shard_map/psum | solution.py:47
  16.1 300.1 %all-reduce.7.cloned.1.call-start = ((), (), s32[]{:S(2)}) async-start(), calls=%async_computation.1 | async-start | bytes 1048576 | tf_op jit(solution)/shard_map/psum | solution.py:30
  173.6 287.9 %all-reduce.9.cloned.1.call-start = ((), (), s32[]{:S(2)}) async-start(), calls=%async_computation.2 | async-start | bytes 196608 | tf_op jit(solution)/shard_map/psum | solution.py:30
  324.4 295.2 %all-reduce.11.cloned.1.call-start = ((), (), s32[]{:S(2)}) async-start(), calls=%async_computation.3 | async-start | bytes 1048576 | tf_op jit(solution)/shard_map/psum | solution.py:30
  467.0 9.8 %copy-start.4 = (f32[1,2,2048]{2,1,0:T(2,128)S(1)}, f32[1,2,2048]{2,1,0:T(2,128)}, u32[]{:S(2)}) copy-start(f32[1,2,2048]{2,1,0:T(2,128)} %param.12) | copy-start | bytes 49156
  467.2 73.2 %copy-start.5 = (f32[2,2048]{1,0:T(2,128)S(1)}, f32[2,2048]{1,0:T(2,128)}, u32[]{:S(2)}) copy-start(f32[2,2048]{1,0:T(2,128)} %param.17) | copy-start | bytes 49156
  467.2 73.2 %copy-start.6 = (f32[2,2048]{1,0:T(2,128)S(1)}, f32[2,2048]{1,0:T(2,128)}, u32[]{:S(2)}) copy-start(f32[2,2048]{1,0:T(2,128)} %param.16) | copy-start | bytes 49156
  625.0 6.5 %copy-start.2 = (f32[2,64,2048]{2,1,0:T(8,128)S(1)}, f32[2,64,2048]{2,1,0:T(8,128)}, u32[]{:S(2)}) copy-start(f32[2,64,2048]{2,1,0:T(8,128)} %param.15) | copy-start | bytes 3145732
  625.0 6.5 %copy-start.3 = (f32[2,64,2048]{2,1,0:T(8,128)S(1)}, f32[2,64,2048]{2,1,0:T(8,128)}, u32[]{:S(2)}) copy-start(f32[2,64,2048]{2,1,0:T(8,128)} %param.14) | copy-start | bytes 3145732
Sparse Core Ops, SparseCore 0:
  16.2 141.5 all-reduce.4
  173.7 142.4 all-reduce.6
  324.6 136.9 all-reduce.8
  476.9 142.6 all-reduce.10
where the time goes:
time: 651 us; the launch traced here: 650 us
  waiting for transfers between devices  499 us (77%)
  blocking collectives  63.6 us (10%)
  matrix products  61.9 us (10%)
  between operations  14.5 us (2%)
  other arithmetic  7.02 us (1%)
    psum x3, waiting for transfers between devices, replicas_total(): return lax.psum(partial_term, ('rep', 'grp'))  357 us
    psum x1, waiting for transfers between devices, local(): p_sum = lax.psum(first_term, ('rep', 'grp'))  141 us
    psum x1, blocking collectives, local(): vec_sum = lax.psum(vec_grads[0], ('rep', 'grp'))  63.6 us
    dot_general x2, matrix products, local(): jnp.einsum('mks,mkd->msd', p_hat, combined, precision=high)  13.4 us
  transfers between devices with their start and end apart: 4, of which 4 were waited for; matrix products, arithmetic and copies ran while one was open for 0% of the time, Pallas kernels for 0%

commit v1 on v0

v1 whole, which is shorter than its diff:
```python
import functools

import jax
import jax.numpy as jnp
from jax import lax
from jax.experimental import pallas as pl
from jax.experimental.pallas import tpu as pltpu
from jax.sharding import PartitionSpec as P

ROOT_ITERS = 12
MESH = pl.DeviceIdType.MESH
HIGH = lax.Precision.HIGHEST
PARTS = 6
SPLITS = 4
SUBS = (32, 24)
STEPS = 2 * SPLITS + 2
CHUNK = 64


def dot(a, b, dims=((1,), (0,))):
    return lax.dot_general(a, b, (dims, ((), ())), precision=HIGH, preferred_element_type=jnp.float32)


def orthonormal(factor):
    rank = factor.shape[0]
    gram = dot(factor, factor, ((1,), (1,)))
    spread = jnp.sqrt(jnp.sum(gram * gram, keepdims=True))
    row = lax.broadcasted_iota(jnp.int32, (rank, rank), 0)
    column = lax.broadcasted_iota(jnp.int32, (rank, rank), 1)
    identity = jnp.where(row == column, 1.0, 0.0).astype(jnp.float32)
    left = gram / spread
    middle = 1.5 * identity - 0.5 * left
    left = dot(left, middle)
    right = middle
    for sweep in range(1, ROOT_ITERS):
        middle = 1.5 * identity - 0.5 * dot(right, left)
        if sweep < ROOT_ITERS - 1:
            left = dot(left, middle)
        right = dot(middle, right)
    return dot(right, factor, ((0,), (0,))) / jnp.sqrt(spread)


def reduce_kernel(grads_ref, errors_ref, warm_ref, vec_ref, q_out, p_out, v_out, *scratch):
    halves = scratch[:SPLITS]
    (
        grads, errors, away, pair, mine, whole0, whole1, middle, total, p_sums, p_recv, q_mine, q_pair, p_mine, p_pair,
        v_pair, load_sem, pair_sem, step_send, step_recv, p_sem, last_sem,
    ) = scratch[SPLITS:]
    core = lax.axis_index("rep") % 2
    place = (lax.axis_index("rep") // 8, (lax.axis_index("rep") // 2) % 4, lax.axis_index("grp"))
    rows, width = errors_ref.shape[2], errors_ref.shape[3]
    high = mine.shape[0]
    tail = high - rows
    count = lax.axis_size("rep") * lax.axis_size("grp")

    def device(x, y, z, c):
        return ((x * 4 + y) * 2 + c, z)

    bits, peers = [], []
    for kind in range(2):
        for axis in range(3):
            at = place[axis]
            moved = list(place)
            moved[axis] = at + 1 - 2 * (at % 2) if kind == 0 else 3 - at
            peers.append(device(*moved, core))
            bits.append((at + at // 2) % 2 if kind == 0 else at // 2)
    partner = device(*place, 1 - core)

    def remote(src, dst, send_sem, recv_sem, to):
        copy = pltpu.make_async_remote_copy(
            src_ref=src, dst_ref=dst, send_sem=send_sem, recv_sem=recv_sem, device_id=to, device_id_type=MESH
        )
        copy.start()
        return copy

    loads = {}
    starts = list(range(0, rows, CHUNK))
    for turn in range(2):
        matrix = 1 - core if turn == 0 else core
        for number, start in enumerate(starts):
            window = pl.ds(start, CHUNK)
            slot = turn * len(starts) + number
            loads[turn, number] = (
                pltpu.make_async_copy(grads_ref.at[0, matrix, window], grads.at[turn, window], load_sem.at[0, slot]),
                pltpu.make_async_copy(errors_ref.at[0, matrix, window], errors.at[turn, window], load_sem.at[1, slot]),
            )
            for copy in loads[turn, number]:
                copy.start()

    barrier = pltpu.get_barrier_semaphore()
    for peer in peers + [partner]:
        pl.semaphore_signal(barrier, inc=1, device_id=peer, device_id_type=MESH)

    first_row = lax.broadcasted_iota(jnp.int32, (tail, width), 0) == 0
    away[rows:, :] = jnp.where(first_row, vec_ref[0, pl.ds(1 - core, 1), :], 0.0)
    mine[rows:, :] = jnp.where(first_row, vec_ref[0, pl.ds(core, 1), :], 0.0)
    pl.semaphore_wait(barrier, len(peers) + 1)

    def combine(turn, number, into):
        for copy in loads[turn, number]:
            copy.wait()
        window = pl.ds(starts[number], CHUNK)
        into[window, :] = grads[turn, window, :].astype(jnp.float32) + errors[turn, window, :]

    sent = []
    handed = []
    for number, start in enumerate(starts):
        combine(0, number, away)
        window = pl.ds(start, CHUNK if number < len(starts) - 1 else CHUNK + tail)
        copy = remote(away.at[window], pair.at[window], pair_sem.at[0, number], pair_sem.at[1, number], partner)
        handed.append(copy)
        sent.append(copy)

    pieces = []
    for sub, size in enumerate(SUBS):
        for part in range(PARTS):
            pieces.append((part, PARTS * sum(SUBS[:sub]) + part * size, size))
    offsets = []
    for part in range(PARTS):
        chain = [0]
        for step in range(SPLITS):
            chain.append(chain[-1] + bits[(part + step) % 6] * (width >> (step + 1)))
        offsets.append(chain)

    def columns(part, depth):
        return pl.ds(pl.multiple_of(offsets[part][depth], 128), width >> depth)

    def others(part, depth):
        half = width >> depth
        begin = offsets[part][depth - 1] + (1 - bits[(part + depth - 1) % 6]) * half
        return pl.ds(pl.multiple_of(begin, 128), half)

    flight = {}

    def begin(step, number):
        part, start, size = pieces[number]
        window = pl.ds(start, size)
        link = (part + (step if step < SPLITS + 2 else STEPS - 1 - step)) % 6
        if step < SPLITS:
            src, dst = mine.at[window, others(part, step + 1)], halves[step].at[window]
        elif step == SPLITS:
            src, dst = mine.at[window, columns(part, SPLITS)], whole0.at[window]
        elif step == SPLITS + 1:
            src, dst = middle.at[window], whole1.at[window]
        else:
            src = dst = total.at[window, columns(part, STEPS - step)]
        flight[step, number] = remote(
            src, dst, step_send.at[step, number], step_recv.at[step, number], peers[link]
        )
        sent.append(flight[step, number])

    def finish(step, number):
        part, start, size = pieces[number]
        window = pl.ds(start, size)
        flight[step, number].wait_recv()
        if step < SPLITS:
            cols = columns(part, step + 1)
            mine[window, cols] = mine[window, cols] + halves[step][window, :]
        elif step == SPLITS:
            middle[window, :] = mine[window, columns(part, SPLITS)] + whole0[window, :]
        elif step == SPLITS + 1:
            total[window, columns(part, SPLITS)] = middle[window, :] + whole1[window, :]

    for number in range(len(starts)):
        combine(1, number, mine)
    for number, start in enumerate(starts):
        handed[number].wait_recv()
        size = CHUNK if number < len(starts) - 1 else CHUNK + tail
        window = pl.ds(start, size)
        mine[window, :] = mine[window, :] + pair[window, :]
        for piece, (part, first, extent) in enumerate(pieces):
            if start < first + extent <= start + size:
                begin(0, piece)

    rank = warm_ref.shape[1]
    live = lax.broadcasted_iota(jnp.int32, (rank, high), 1) < rows
    p_sums[0] = jnp.where(live, dot(warm_ref[core], mine[...], ((1,), (1,))), 0.0)
    p_flight = None
    for step in range(STEPS):
        if step < 6:
            p_flight = remote(p_sums.at[step], p_recv.at[step], p_sem.at[0, step], p_sem.at[1, step], peers[step])
            sent.append(p_flight)
        for number in range(len(pieces)):
            finish(step, number)
            if step < STEPS - 1:
                begin(step + 1, number)
        if step < 6:
            p_flight.wait_recv()
            p_sums[step + 1] = p_sums[step] + p_recv[step]
        if step == STEPS - 2:
            p_hat = orthonormal(p_sums[6] / count)
    v_copy = remote(total.at[pl.ds(rows, 8)], v_pair, last_sem.at[0, 0], last_sem.at[1, 0], partner)
    q_factor = dot(p_hat, total[...]) / count
    p_sum = jnp.where(live, dot(q_factor, total[...], ((1,), (1,))), 0.0)
    p_hat = orthonormal(p_sum / count)
    p_mine[...] = p_hat
    p_copy = remote(p_mine, p_pair, last_sem.at[0, 1], last_sem.at[1, 1], partner)
    q_mine[...] = dot(p_hat, total[...]) / count
    q_copy = remote(q_mine, q_pair, last_sem.at[0, 2], last_sem.at[1, 2], partner)
    v_out[core] = total[rows : rows + 8, :] / count
    p_out[core] = p_mine[...].T[:rows]
    q_out[core] = q_mine[...]
    v_copy.wait_recv()
    v_out[1 - core] = v_pair[...] / count
    p_copy.wait_recv()
    p_out[1 - core] = p_pair[...].T[:rows]
    q_copy.wait_recv()
    q_out[1 - core] = q_pair[...]
    for copy in sent + [v_copy, p_copy, q_copy]:
        copy.wait_send()


def apply_kernel(
    owners, grads, errors, p_hat, q_factor, vec_avg, mat_m, mat_w, vec_m, vec_w,
    new_errors, mat_m_out, mat_w_out, vec_m_out, vec_w_out,
):
    step = pl.program_id(0)
    device = lax.axis_index("rep") * lax.axis_size("grp") + lax.axis_index("grp")
    items = owners.shape[0]
    heads = items - vec_m.shape[0]

    def home(item):
        owner = owners[item]
        slot = jnp.int32(0)
        for before in range(items):
            slot += jnp.where((before < item) & (owners[before] == owner), 1, 0)
        return owner == device, slot

    @pl.when(step == 0)
    def _():
        mat_m_out[...] = mat_m[...]
        mat_w_out[...] = mat_w[...]
        vec_m_out[...] = vec_m[...]
        vec_w_out[...] = vec_w[...]
        for gain in range(items - heads):
            here, slot = home(heads + gain)

            @pl.when(here)
            def _():
                moment = 0.9 * vec_m[pl.ds(slot, 1), :] + vec_avg[gain, :1, :]
                vec_m_out[pl.ds(slot, 1), :] = moment
                vec_w_out[pl.ds(slot, 1), :] = vec_w[pl.ds(slot, 1), :] - 0.5 * moment

    approx = dot(p_hat[0], q_factor[0])
    new_errors[0, 0] = grads[0, 0].astype(jnp.float32) + errors[0, 0] - approx
    here, slot = home(step)

    @pl.when(here)
    def _():
        moment = 0.9 * mat_m[slot] + approx
        mat_m_out[slot] = moment
        mat_w_out[slot] = mat_w[slot] - 0.5 * moment


def local(grads, errors, warm_start, vec_grads, owners, mat_momentum, mat_weights, vec_momentum, vec_weights):
    _, matrices, rows, width = errors.shape
    rank = warm_start.shape[1]
    high = PARTS * sum(SUBS)
    f32 = jnp.float32
    pieces = PARTS * len(SUBS)
    vmem = pl.BlockSpec(memory_space=pltpu.VMEM)
    hbm = pl.BlockSpec(memory_space=pl.ANY)
    dma = pltpu.SemaphoreType.DMA
    q_factor, p_hat, vec_avg = pl.pallas_call(
        reduce_kernel,
        out_shape=(
            jax.ShapeDtypeStruct((matrices, rank, width), f32),
            jax.ShapeDtypeStruct((matrices, rows, rank), f32),
            jax.ShapeDtypeStruct((matrices, 8, width), f32),
        ),
        in_specs=[hbm, hbm, vmem, vmem],
        out_specs=(vmem, vmem, vmem),
        scratch_shapes=[pltpu.VMEM((high, width >> (step + 1)), f32) for step in range(SPLITS)]
        + [
            pltpu.VMEM((2, rows, width), jnp.bfloat16),
            pltpu.VMEM((2, rows, width), f32),
            pltpu.VMEM((high, width), f32),
            pltpu.VMEM((high, width), f32),
            pltpu.VMEM((high, width), f32),
            pltpu.VMEM((high, width >> SPLITS), f32),
            pltpu.VMEM((high, width >> SPLITS), f32),
            pltpu.VMEM((high, width >> SPLITS), f32),
            pltpu.VMEM((high, width), f32),
            pltpu.VMEM((7, rank, high), f32),
            pltpu.VMEM((6, rank, high), f32),
            pltpu.VMEM((rank, width), f32),
            pltpu.VMEM((rank, width), f32),
            pltpu.VMEM((rank, high), f32),
            pltpu.VMEM((rank, high), f32),
            pltpu.VMEM((8, width), f32),
            dma((2, 2 * (rows // CHUNK))),
            dma((2, rows // CHUNK)),
            dma((STEPS, pieces)),
            dma((STEPS, pieces)),
            dma((2, 6)),
            dma((2, 3)),
        ],
        compiler_params=pltpu.CompilerParams(
            collective_id=0, has_side_effects=True, vmem_limit_bytes=60 * 1024 * 1024
        ),
        name="reduce",
    )(grads, errors, warm_start, vec_grads)

    heads = rows // mat_momentum.shape[1]
    head = mat_momentum.shape[1]
    slots = mat_momentum.shape[0]
    block = pl.BlockSpec((1, 1, head, width), lambda i, owners: (0, i // heads, i % heads, 0))

    def fixed(*shape):
        return pl.BlockSpec(shape, lambda i, owners: (0,) * len(shape))

    mats, vecs = fixed(slots, head, width), fixed(slots, width)
    return pl.pallas_call(
        apply_kernel,
        out_shape=(
            jax.ShapeDtypeStruct(errors.shape, f32),
            jax.ShapeDtypeStruct(mat_momentum.shape, f32),
            jax.ShapeDtypeStruct(mat_weights.shape, f32),
            jax.ShapeDtypeStruct(vec_momentum.shape, f32),
            jax.ShapeDtypeStruct(vec_weights.shape, f32),
        ),
        grid_spec=pltpu.PrefetchScalarGridSpec(
            num_scalar_prefetch=1,
            grid=(matrices * heads,),
            in_specs=[
                block,
                block,
                pl.BlockSpec((1, head, rank), lambda i, owners: (i // heads, i % heads, 0)),
                pl.BlockSpec((1, rank, width), lambda i, owners: (i // heads, 0, 0)),
                fixed(matrices, 8, width),
                mats,
                mats,
                vecs,
                vecs,
            ],
            out_specs=(block, mats, mats, vecs, vecs),
        ),
        name="apply",
    )(owners, grads, errors, p_hat, q_factor, vec_avg, mat_momentum, mat_weights, vec_momentum, vec_weights)


def solution(mesh):
    both = ("rep", "grp")
    placed = (
        P(both, None, None, None), P(both, None, None, None), P(), P(both, None, None), P(),
        P(both, None, None), P(both, None, None), P(both, None), P(both, None),
    )
    return jax.shard_map(
        local,
        mesh=mesh,
        in_specs=placed,
        out_specs=(P(both, None, None, None), P(both, None, None), P(both, None, None), P(both, None), P(both, None)),
        check_vma=False,
    )
```

time: 651 us -> 82.9 us (0.13)
  waiting for transfers between devices: 499 us -> 0 us
  Pallas kernels: 0 us -> 81.9 us
  blocking collectives: 63.6 us -> 0 us
  matrix products: 61.9 us -> 0 us
  between operations: 14.5 us -> 0.64 us
  other arithmetic: 7.02 us -> 0 us
    psum x4 -> x0, waiting for transfers between devices: 499 us -> none  [the longest x3 357 us: replicas_total(): return lax.psum(partial_term, ('rep', 'grp'))]
    pallas_call x0 -> x2, Pallas kernels: none -> 81.9 us  [the longest x1 68.4 us: local(): pl.pallas_call(reduce_kernel, out_shape=(jax.ShapeDtypeStruct((matrices,...]
    psum x1 -> x0, blocking collectives: 63.6 us -> none  [local(): vec_sum = lax.psum(vec_grads[0], ('rep', 'grp'))]
    dot_general x81 -> x0, matrix products: 61.9 us -> none  [the longest x2 13.4 us: local(): jnp.einsum('mks,mkd->msd', p_hat, combined, precision=high)]
  transfers between devices with their start and end apart: 4 -> 0, of which waited for: 4 -> 0; matrix products, arithmetic and copies ran while one was open for 0% -> 0% of each run, Pallas kernels for 0% -> 0%
where the time goes in v1:
time: 82.9 us; the launch traced here: 82.6 us
  Pallas kernels  81.9 us (99%)
    pallas_call x1, Pallas kernels, local(): pl.pallas_call(reduce_kernel, out_shape=(jax.ShapeDtypeStruct((matrices,...  68.4 us
    pallas_call x1, Pallas kernels, local(): pl.pallas_call(apply_kernel, out_shape=(jax.ShapeDtypeStruct(errors.shape...  13.6 us

profile of v1, /device:TPU:1, one launch (start us, length us, event | category | flops | bytes accessed | tf_op | source)
XLA Modules:
  0.0 82.6 jit_solution(15147779512067268062)
XLA Ops:
  0.6 68.4 %reduce.1 = (f32[2,32,2048]{2,1,0:T(8,128)}, f32[2,320,32]{2,1,0:T(8,128)}, f32[2,8,2048]{2,1,0:T(8,128)}) custom-call(bf16[1,2,320,2048]{3,2,1,0:T(8,128)(2,1)} %grads.1, f32[1,2,320,2048]{3,2,1,0:T(8,128)} %errors.1, f32[2,32,2048]{2,1,0:T(8,128)} %warm_ref.1, f32[1,2,2048]{2,1,0:T(2,128)} %vec_ref.1), custom_call_target="tpu_custom_call" | custom-call | tf_op jit(solution)/shard_map/reduce/pallas_call | solution.py:264
  69.0 13.6 %apply.1 = (f32[1,2,320,2048]{3,2,1,0:T(8,128)}, f32[2,64,2048]{2,1,0:T(8,128)}, f32[2,64,2048]{2,1,0:T(8,128)}, f32[2,2048]{1,0:T(2,128)}, f32[2,2048]{1,0:T(2,128)}) custom-call(s32[12]{0:T(128)} %owners.1, bf16[1,2,320,2048]{3,2,1,0:T(8,128)(2,1)} %grads.1, f32[1,2,320,2048]{3,2,1,0:T(8,128)} %errors.1, f32[2,320,32]{2,1,0:T(8,128)} %get-tuple-element.8.p_hat, ...), custom_call_target="tpu_custom_call" | custom-call | tf_op jit(solution)/shard_map/apply/pallas_call | solution.py:313

commit v2 on v1

--- a/solution.py
+++ b/solution.py
@@ -19,6 +19,20 @@
 
 def dot(a, b, dims=((1,), (0,))):
     return lax.dot_general(a, b, (dims, ((), ())), precision=HIGH, preferred_element_type=jnp.float32)
+
+
+def split(value):
+    coarse = value.astype(jnp.bfloat16)
+    return coarse, (value - coarse.astype(jnp.float32)).astype(jnp.bfloat16)
+
+
+def split_dot(a, b, dims=((1,), (0,))):
+    def one(left, right):
+        return lax.dot_general(left, right, (dims, ((), ())), preferred_element_type=jnp.float32)
+
+    coarse, fine = split(a)
+    both = one(jnp.concatenate([coarse, fine], axis=0), b[0])
+    return both[: a.shape[0]] + (both[a.shape[0] :] + one(coarse, b[1]))
 
 
 def orthonormal(factor):
@@ -174,7 +188,7 @@
 
     rank = warm_ref.shape[1]
     live = lax.broadcasted_iota(jnp.int32, (rank, high), 1) < rows
-    p_sums[0] = jnp.where(live, dot(warm_ref[core], mine[...], ((1,), (1,))), 0.0)
+    p_sums[0] = jnp.where(live, split_dot(warm_ref[core], split(mine[...]), ((1,), (1,))), 0.0)
     p_flight = None
     for step in range(STEPS):
         if step < 6:
@@ -190,12 +204,13 @@
         if step == STEPS - 2:
             p_hat = orthonormal(p_sums[6] / count)
     v_copy = remote(total.at[pl.ds(rows, 8)], v_pair, last_sem.at[0, 0], last_sem.at[1, 0], partner)
-    q_factor = dot(p_hat, total[...]) / count
-    p_sum = jnp.where(live, dot(q_factor, total[...], ((1,), (1,))), 0.0)
+    parts = split(total[...])
+    q_factor = split_dot(p_hat, parts) / count
+    p_sum = jnp.where(live, split_dot(q_factor, parts, ((1,), (1,))), 0.0)
     p_hat = orthonormal(p_sum / count)
     p_mine[...] = p_hat
     p_copy = remote(p_mine, p_pair, last_sem.at[0, 1], last_sem.at[1, 1], partner)
-    q_mine[...] = dot(p_hat, total[...]) / count
+    q_mine[...] = split_dot(p_hat, parts) / count
     q_copy = remote(q_mine, q_pair, last_sem.at[0, 2], last_sem.at[1, 2], partner)
     v_out[core] = total[rows : rows + 8, :] / count
     p_out[core] = p_mine[...].T[:rows]
@@ -241,7 +256,7 @@
                 vec_m_out[pl.ds(slot, 1), :] = moment
                 vec_w_out[pl.ds(slot, 1), :] = vec_w[pl.ds(slot, 1), :] - 0.5 * moment
 
-    approx = dot(p_hat[0], q_factor[0])
+    approx = split_dot(p_hat[0], split(q_factor[0]))
     new_errors[0, 0] = grads[0, 0].astype(jnp.float32) + errors[0, 0] - approx
     here, slot = home(step)
 

time: 82.9 us -> 77.3 us (0.932)
  Pallas kernels: 81.9 us -> 76.3 us
    pallas_call x1, Pallas kernels: 68.4 us -> 63.9 us  [local(): pl.pallas_call(reduce_kernel, out_shape=(jax.ShapeDtypeStruct((matrices,...]
    pallas_call x1, Pallas kernels: 13.6 us -> 12.4 us  [local(): pl.pallas_call(apply_kernel, out_shape=(jax.ShapeDtypeStruct(errors.shape...]
where the time goes in v2:
time: 77.3 us; the launch traced here: 76.9 us
  Pallas kernels  76.3 us (99%)
    pallas_call x1, Pallas kernels, local(): pl.pallas_call(reduce_kernel, out_shape=(jax.ShapeDtypeStruct((matrices,...  63.9 us
    pallas_call x1, Pallas kernels, local(): pl.pallas_call(apply_kernel, out_shape=(jax.ShapeDtypeStruct(errors.shape...  12.4 us

profile of v2, /device:TPU:1, one launch (start us, length us, event | category | flops | bytes accessed | tf_op | source)
XLA Modules:
  0.0 76.9 jit_solution(3615570934611737590)
XLA Ops:
  0.6 63.9 %reduce.1 = (f32[2,32,2048]{2,1,0:T(8,128)}, f32[2,320,32]{2,1,0:T(8,128)}, f32[2,8,2048]{2,1,0:T(8,128)}) custom-call(bf16[1,2,320,2048]{3,2,1,0:T(8,128)(2,1)} %grads.1, f32[1,2,320,2048]{3,2,1,0:T(8,128)} %errors.1, f32[2,32,2048]{2,1,0:T(8,128)} %warm_ref.1, f32[1,2,2048]{2,1,0:T(2,128)} %vec_ref.1), custom_call_target="tpu_custom_call" | custom-call | tf_op jit(solution)/shard_map/reduce/pallas_call | solution.py:279
  64.6 12.4 %apply.1 = (f32[1,2,320,2048]{3,2,1,0:T(8,128)}, f32[2,64,2048]{2,1,0:T(8,128)}, f32[2,64,2048]{2,1,0:T(8,128)}, f32[2,2048]{1,0:T(2,128)}, f32[2,2048]{1,0:T(2,128)}) custom-call(s32[12]{0:T(128)} %owners.1, bf16[1,2,320,2048]{3,2,1,0:T(8,128)(2,1)} %grads.1, f32[1,2,320,2048]{3,2,1,0:T(8,128)} %errors.1, f32[2,320,32]{2,1,0:T(8,128)} %get-tuple-element.8.p_hat, ...), custom_call_target="tpu_custom_call" | custom-call | tf_op jit(solution)/shard_map/apply/pallas_call | solution.py:328
